TPU v7x, 32 devices: a whole 2x2x4 slice. The times are simulated.
32 devices in a mesh: gx: 8 (over z, y), gy: 4 (over x, core).
Axes of the slice: x: 2, y: 2, z: 4, core: 2. Of those that a mesh axis runs over, the one named last changes fastest.
Arguments:
- right_side: float32 [64, 128, 128], P('gy', 'gx'), may hold values from -6 to 9
- diagonal: float32 [64, 128, 128], P('gy', 'gx'), may hold values from 0.02 to 0.5
- horizontal: float32 [64, 128, 128], P('gy', 'gx'), may hold values from 0.1 to 1
- vertical: float32 [128], replicated, may hold values from 0.2 to 2
- precond: float32 [2, 128, 128], replicated, may hold values from -4 to 4
- edge_rows: int32 [2, 64], replicated, may hold values from 0 to 63, as said below
Outputs:
- solution_field: float32 [64, 128, 128], P('gy', 'gx')
- residual: float32 [64, 128, 128], P('gy', 'gx')
- residual_sq: float32 [3], replicated
Inputs may be any that keep to these rules, and one draw needn't show every extreme that they name: Each row of edge_rows lists every number 0 to 63 exactly once.
All inputs are finite; a program needn't handle non-finite values.
Results may differ from a plain program's by a relative error of at most 0.00014.
Values sent between devices are 32-bit elements; how exact they have to be, the bound alone decides.
No kernel may reach another device: no remote copies, remote signals or barrier semaphores. Data moves between devices by JAX's collectives and lax.ppermute only.
A program may use at most 64 MiB of HBM per device.

v0:
```python
import jax
import jax.numpy as jnp
from jax import lax
from jax.sharding import PartitionSpec as P

ITERS = 3


def padded(x, sides, width, wrap):
    for axis, dim in sides:
        devices, length = (lax.axis_size(axis), x.shape[dim])
        up = [(i, (i + 1) % devices) for i in range(devices if wrap else devices - 1)]
        down = [(j, i) for i, j in up]
        last = lax.slice_in_dim(x, length - width, length, axis=dim)
        initial = lax.slice_in_dim(x, 0, width, axis=dim)
        before = lax.ppermute(last, axis, up)
        after = lax.ppermute(initial, axis, down)
        x = jnp.concatenate([before, x, after], axis=dim)
    return x


def local_product(left, right):
    return jnp.sum(left * right)


def on_device(right_side, diagonal, horizontal, vertical, precond, edge_rows):
    rows, cols, levels = right_side.shape
    n_gx = lax.axis_size("gx")
    n_gy = lax.axis_size("gy")
    col_index = lax.axis_index("gx")
    row_index = lax.axis_index("gy")
    total_cells = float(rows * cols * levels * n_gx * n_gy)
    half = n_gx // 2
    panel = (col_index >= half).astype(jnp.int32)
    matrix = lax.dynamic_index_in_dim(precond, panel, 0, keepdims=False)
    east_table = jnp.where(col_index == half - 1, edge_rows[0], edge_rows[1])
    west_table = jnp.where(col_index == half, edge_rows[0], edge_rows[1])
    first_row = row_index * rows
    east_local = lax.dynamic_slice_in_dim(east_table, first_row, rows)
    west_local = lax.dynamic_slice_in_dim(west_table, first_row, rows)
    east_border = (col_index == half - 1) | (col_index == n_gx - 1)
    west_border = (col_index == half) | (col_index == 0)
    solution_field = jnp.zeros_like(right_side)
    residual = right_side
    directions = []
    images = []
    norms = []
    for step in range(ITERS):
        pre = jnp.einsum("yxl,kl->yxk", residual, matrix, precision=lax.Precision.HIGHEST)
        wide = padded(pre, (("gx", 1),), 1, True)
        edges = jnp.stack([wide[:, 0], wide[:, -1]], 0)
        whole = lax.all_gather(edges, "gy", axis=1, tiled=True)
        west_fix = jnp.take(whole[0], west_local, axis=0)
        east_fix = jnp.take(whole[1], east_local, axis=0)
        west = jnp.where(west_border, west_fix, edges[0])
        east = jnp.where(east_border, east_fix, edges[1])
        tall = padded(pre, (("gy", 0),), 1, False)
        flat = jnp.pad(pre, ((0, 0), (0, 0), (1, 1)))
        east_side = jnp.concatenate([pre[:, 1:], east[:, None]], 1)
        west_side = jnp.concatenate([west[:, None], pre[:, :-1]], 1)
        beside = east_side + west_side + tall[2:] + tall[:-2]
        column = flat[:, :, 2:] + flat[:, :, :-2]
        image = diagonal * pre + horizontal * (4.0 * pre - beside) + vertical * (2.0 * pre - column)
        count = len(images)
        terms = [local_product(image, older) for older in images]
        terms = terms + [local_product(residual, older) for older in images]
        terms = terms + [local_product(image, image), local_product(residual, image)]
        if step > 0:
            terms.append(local_product(residual, residual))
        totals = lax.psum(jnp.stack(terms), ("gx", "gy")) / total_cells
        coeffs = totals[:count]
        against = totals[count : 2 * count]
        square = totals[2 * count] - jnp.sum(coeffs * coeffs)
        along = totals[2 * count + 1] - jnp.sum(coeffs * against)
        if step > 0:
            norms.append(totals[2 * count + 2])
        for number in range(count):
            pre = pre - coeffs[number] * directions[number]
            image = image - coeffs[number] * images[number]
        scale = 1.0 / jnp.sqrt(square)
        alpha = along * scale
        direction = pre * scale
        image = image * scale
        solution_field = solution_field + alpha * direction
        residual = residual - alpha * image
        directions.append(direction)
        images.append(image)
    norms.append(lax.psum(local_product(residual, residual), ("gx", "gy")) / total_cells)
    return (solution_field, residual, jnp.stack(norms))


def solution(mesh):
    in_specs = (P("gy", "gx", None), P("gy", "gx", None), P("gy", "gx", None), P(), P(), P())
    out_specs = (P("gy", "gx", None), P("gy", "gx", None), P())
    return jax.shard_map(
        on_device, mesh=mesh, in_specs=in_specs, out_specs=out_specs, check_vma=False
    )
```

profile of v0, /device:TPU:0, one launch (start us, length us, event | category | flops | bytes accessed | tf_op | source)
XLA Modules:
  0.0 243.0 jit_solution(2497374235617542815)
XLA Ops:
  0.6 0.0 copy-start
  0.7 0.9 copy-done
  1.5 1.2 convolution_bitcast_fusion
  2.7 1.3 collective-permute-start.2
  4.0 3.0 %collective-permute-start.3 = (f32[1,16,128]{2,1,0:T(8,128)S(1)}, f32[1,16,128]{2,1,0:T(8,128)S(1)}, u32[]{:S(2)}, u32[]{:S(2)}) collective-permute-start(f32[1,16,128]{2,1,0:T(8,128)S(1)} %get-tuple-element.48), channel_id=1, source_target_pairs={{0,1},{1,2},{2,3},{4,5},{5,6},{6,7},{8,9},{9,10},{10,11},{12,13},{... | collective-permute-start | bytes 24584 | tf_op jit(solution)/shard_map/ppermute | solution.py:16
  7.1 3.0 %collective-permute-start = (f32[16,1,128]{2,0,1:T(8,128)S(1)}, f32[16,1,128]{2,0,1:T(8,128)S(1)}, u32[]{:S(2)}, u32[]{:S(2)}) collective-permute-start(f32[16,1,128]{2,0,1:T(8,128)S(1)} %bitcast.112), channel_id=1, source_target_pairs={{0,4},{4,8},{8,12},{12,16},{16,20},{20,24},{24,28},{28,0},{1,5},{5... | collective-permute-start | bytes 24584 | tf_op jit(solution)/shard_map/ppermute | solution.py:16
  10.1 3.1 %collective-permute-start.1 = (f32[16,1,128]{2,0,1:T(8,128)S(1)}, f32[16,1,128]{2,0,1:T(8,128)S(1)}, u32[]{:S(2)}, u32[]{:S(2)}) collective-permute-start(f32[16,1,128]{2,0,1:T(8,128)S(1)} %bitcast.111), channel_id=1, source_target_pairs={{4,0},{8,4},{12,8},{16,12},{20,16},{24,20},{28,24},{0,28},{5,1},{9... | collective-permute-start | bytes 24584 | tf_op jit(solution)/shard_map/ppermute | solution.py:17
  13.3 0.0 copy-start.5
  13.3 0.7 copy-done.5
  14.0 0.1 compare_and_fusion.1
  14.0 0.1 compare_and_fusion
  14.2 0.7 collective-permute-done
  14.8 0.0 collective-permute-done.1
  14.8 5.4 %all_gather.9 = f32[2,64,128]{2,1,0:T(8,128)S(1)} all-gather(f32[2,16,128]{2,1,0:T(8,128)S(1)} %pad_maximum_fusion.6), channel_id=1, replica_groups=mesh['gx'=8,'gy'=4] {'gy'}, dimensions={1}, use_global_device_ids=true | all-gather | bytes 81920 | tf_op jit(solution)/shard_map/all_gather | solution.py:52
  20.2 0.6 gather_fusion
  20.8 0.6 gather_fusion.1
  21.3 0.1 bitcast_select_fusion.5
  21.4 0.1 bitcast_select_fusion.4
  21.5 0.0 collective-permute-done.2
  21.5 0.0 collective-permute-done.3
  21.5 0.0 copy-start.4
  21.5 0.6 copy-done.4
  22.2 0.7 multiply_reduce_fusion.14
  22.9 1.4 pad_maximum_fusion.9
  24.3 40.2 %psum.28 = f32[2]{0:T(128)S(1)} all-reduce(f32[2]{0:T(128)S(1)} %pad_maximum_fusion.9), channel_id=1, replica_groups=mesh['gx'=8,'gy'=4] {'gx','gy'}, use_global_device_ids=true, to_apply=%region_2.4 | all-reduce | flops 2 | bytes 16 | tf_op jit(solution)/shard_map/psum | solution.py:70
  64.5 0.6 fusion.54
  66.5 0.3 fusion.29
  66.8 2.3 collective-permute-start.4
  69.1 2.5 %collective-permute-start.5 = (f32[16,1,128]{2,0,1:T(8,128)S(1)}, f32[16,1,128]{2,0,1:T(8,128)S(1)}, u32[]{:S(2)}, u32[]{:S(2)}) collective-permute-start(f32[16,1,128]{2,0,1:T(8,128)S(1)} %bitcast.113), channel_id=1, source_target_pairs={{4,0},{8,4},{12,8},{16,12},{20,16},{24,20},{28,24},{0,28},{5,1},{9... | collective-permute-start | bytes 24584 | tf_op jit(solution)/shard_map/ppermute | solution.py:17
  71.6 1.3 collective-permute-start.6
  72.9 3.0 %collective-permute-start.7 = (f32[1,16,128]{2,1,0:T(8,128)S(1)}, f32[1,16,128]{2,1,0:T(8,128)S(1)}, u32[]{:S(2)}, u32[]{:S(2)}) collective-permute-start(f32[1,16,128]{2,1,0:T(8,128)S(1)} %get-tuple-element.42), channel_id=1, source_target_pairs={{0,1},{1,2},{2,3},{4,5},{5,6},{6,7},{8,9},{9,10},{10,11},{12,13},{... | collective-permute-start | bytes 24584 | tf_op jit(solution)/shard_map/ppermute | solution.py:16
  75.9 0.0 collective-permute-done.4
  75.9 0.0 collective-permute-done.5
  75.9 5.8 %all_gather.10 = f32[2,64,128]{2,1,0:T(8,128)S(1)} all-gather(f32[2,16,128]{2,1,0:T(8,128)S(1)} %pad_maximum_fusion.7), channel_id=1, replica_groups=mesh['gx'=8,'gy'=4] {'gy'}, dimensions={1}, use_global_device_ids=true | all-gather | bytes 81920 | tf_op jit(solution)/shard_map/all_gather | solution.py:52
  81.8 0.6 gather_fusion.2
  82.3 0.6 gather_fusion.3
  82.9 0.1 bitcast_select_fusion.3
  83.0 0.1 bitcast_select_fusion.2
  83.0 0.0 collective-permute-done.6
  83.0 0.0 collective-permute-done.7
  83.1 0.8 multiply_reduce_fusion.8
  83.8 3.2 %stack.76 = f32[5]{0:T(128)S(1)} concatenate(f32[1]{0:T(128)} %bitcast.28, f32[1]{0:T(128)} %bitcast.29, f32[1]{0:T(128)} %bitcast.30, f32[1]{0:T(128)} %bitcast.31, f32[1]{0:T(128)} %bitcast.32), dimensions={0} | concatenate | bytes 40 | tf_op jit(solution)/shard_map/stack | solution.py:70
  87.1 37.9 %psum.29 = f32[5]{0:T(128)S(1)} all-reduce(f32[5]{0:T(128)S(1)} %stack.76), channel_id=1, replica_groups=mesh['gx'=8,'gy'=4] {'gx','gy'}, use_global_device_ids=true, to_apply=%region_8.10 | all-reduce | flops 5 | bytes 40 | tf_op jit(solution)/shard_map/psum | solution.py:70
  124.9 0.6 fusion.52
  129.4 0.7 multiply_subtract_fusion.1
  130.1 0.3 fusion.27
  130.4 2.3 collective-permute-start.8
  132.7 2.5 %collective-permute-start.9 = (f32[16,1,128]{2,0,1:T(8,128)S(1)}, f32[16,1,128]{2,0,1:T(8,128)S(1)}, u32[]{:S(2)}, u32[]{:S(2)}) collective-permute-start(f32[16,1,128]{2,0,1:T(8,128)S(1)} %bitcast.114), channel_id=1, source_target_pairs={{4,0},{8,4},{12,8},{16,12},{20,16},{24,20},{28,24},{0,28},{5,1},{9... | collective-permute-start | bytes 24584 | tf_op jit(solution)/shard_map/ppermute | solution.py:17
  135.2 1.3 collective-permute-start.10
  136.5 3.0 %collective-permute-start.11 = (f32[1,16,128]{2,1,0:T(8,128)S(1)}, f32[1,16,128]{2,1,0:T(8,128)S(1)}, u32[]{:S(2)}, u32[]{:S(2)}) collective-permute-start(f32[1,16,128]{2,1,0:T(8,128)S(1)} %get-tuple-element.36), channel_id=1, source_target_pairs={{0,1},{1,2},{2,3},{4,5},{5,6},{6,7},{8,9},{9,10},{10,11},{12,13},{... | collective-permute-start | bytes 24584 | tf_op jit(solution)/shard_map/ppermute | solution.py:16
  139.6 5.8 %all_gather.11 = f32[2,64,128]{2,1,0:T(8,128)S(1)} all-gather(f32[2,16,128]{2,1,0:T(8,128)S(1)} %pad_maximum_fusion.8), channel_id=1, replica_groups=mesh['gx'=8,'gy'=4] {'gy'}, dimensions={1}, use_global_device_ids=true | all-gather | bytes 81920 | tf_op jit(solution)/shard_map/all_gather | solution.py:52
  145.4 0.6 gather_fusion.4
  145.9 0.6 gather_fusion.5
  146.5 0.1 bitcast_select_fusion.1
  146.6 0.1 bitcast_select_fusion
  146.7 0.9 multiply_reduce_fusion.1
  147.5 4.5 %stack.85 = f32[7]{0:T(128)S(1)} concatenate(f32[1]{0:T(128)} %bitcast.46, f32[1]{0:T(128)} %bitcast.47, f32[1]{0:T(128)} %bitcast.48, f32[1]{0:T(128)} %bitcast.49, f32[1]{0:T(128)} %bitcast.50, f32[1]{0:T(128)} %bitcast.51, f32[1]{0:T(128)} %bitcast.52), dimensions={0} | concatenate | bytes 56 | tf_op jit(solution)/shard_map/stack | solution.py:70
  152.0 38.1 %psum.30 = f32[7]{0:T(128)S(1)} all-reduce(f32[7]{0:T(128)S(1)} %stack.85), channel_id=1, replica_groups=mesh['gx'=8,'gy'=4] {'gx','gy'}, use_global_device_ids=true, to_apply=%region_16.18 | all-reduce | flops 7 | bytes 56 | tf_op jit(solution)/shard_map/psum | solution.py:70
  190.1 0.8 multiply_reduce_fusion.16
  190.9 0.7 fusion.53
  194.1 2.6 %multiply_add_fusion = f32[16,16,128]{2,1,0:T(8,128)} fusion(f32[16,16,128]{2,1,0:T(8,128)S(1)} %fusion.27, f32[16,16,128]{2,1,0:T(8,128)S(1)} %fusion.29, f32[16,16,128]{2,1,0:T(8,128)S(1)} %convolution_bitcast_fusion, f32[]{:T(128)S(6)} %sqrt.17, f32[]{:T(128)} %bitcast.56, f32[]{:T(128)} %bitcast.55, f32[]{:T(128)S(6)} %mul.267, f32[]{:T(128)} %bitcast.34, ...), kind=kLoop, calls=%fused_computation.51 | loop fusion | flops 458752 | bytes 524324 | tf_op jit(solution)/shard_map/add | solution.py:84
  196.7 2.5 %multiply_reduce_fusion = (f32[]{:T(128)}, f32[16,16,128]{2,1,0:T(8,128)}) fusion(f32[16,16,128]{2,1,0:T(8,128)S(1)} %get-tuple-element.23, f32[]{:T(128)S(6)} %sqrt.17, f32[16,16,128]{2,1,0:T(8,128)S(1)} %get-tuple-element.24, f32[]{:T(128)} %bitcast.56, f32[16,16,128]{2,1,0:T(8,128)S(1)} %get-tuple-element.22, f32[16,16,128]{2,1,0:T(8,128)S(1)} %get-tuple-element.26, ...), kind=kLoop, calls=%fused_computation.49 | loop fusion | flops 327679 | bytes 655384 | tf_op jit(solution)/shard_map/reduce_sum | solution.py:23
  199.2 41.3 %psum.31 = f32[]{:T(128)} all-reduce(f32[]{:T(128)} %get-tuple-element.20), channel_id=1, replica_groups=mesh['gx'=8,'gy'=4] {'gx','gy'}, use_global_device_ids=true, to_apply=%region_20.22 | all-reduce | flops 1 | bytes 8 | tf_op jit(solution)/shard_map/psum | solution.py:88
  241.2 1.8 pad_maximum_fusion.10
  (32 shorter events, 0.2 us)
Async XLA Ops:
  0.6 0.9 copy-start
  2.7 18.8 %collective-permute-start.2 = (f32[1,16,128]{2,1,0:T(8,128)S(1)}, f32[1,16,128]{2,1,0:T(8,128)S(1)}, u32[]{:S(2)}, u32[]{:S(2)}) collective-permute-start(f32[1,16,128]{2,1,0:T(8,128)S(1)} %get-tuple-element.47), channel_id=1, source_target_pairs={{1,0},{2,1},{3,2},{5,4},{6,5},{7,6},{9,8},{10,9},{11,10},{13,12},{... | collective-permute-start | bytes 24584 | tf_op jit(solution)/shard_map/ppermute | solution.py:17
  4.0 17.5 %collective-permute-start.3 = (f32[1,16,128]{2,1,0:T(8,128)S(1)}, f32[1,16,128]{2,1,0:T(8,128)S(1)}, u32[]{:S(2)}, u32[]{:S(2)}) collective-permute-start(f32[1,16,128]{2,1,0:T(8,128)S(1)} %get-tuple-element.48), channel_id=1, source_target_pairs={{0,1},{1,2},{2,3},{4,5},{5,6},{6,7},{8,9},{9,10},{10,11},{12,13},{... | collective-permute-start | bytes 24584 | tf_op jit(solution)/shard_map/ppermute | solution.py:16
  7.1 7.7 %collective-permute-start = (f32[16,1,128]{2,0,1:T(8,128)S(1)}, f32[16,1,128]{2,0,1:T(8,128)S(1)}, u32[]{:S(2)}, u32[]{:S(2)}) collective-permute-start(f32[16,1,128]{2,0,1:T(8,128)S(1)} %bitcast.112), channel_id=1, source_target_pairs={{0,4},{4,8},{8,12},{12,16},{16,20},{20,24},{24,28},{28,0},{1,5},{5... | collective-permute-start | bytes 24584 | tf_op jit(solution)/shard_map/ppermute | solution.py:16
  10.1 4.7 %collective-permute-start.1 = (f32[16,1,128]{2,0,1:T(8,128)S(1)}, f32[16,1,128]{2,0,1:T(8,128)S(1)}, u32[]{:S(2)}, u32[]{:S(2)}) collective-permute-start(f32[16,1,128]{2,0,1:T(8,128)S(1)} %bitcast.111), channel_id=1, source_target_pairs={{4,0},{8,4},{12,8},{16,12},{20,16},{24,20},{28,24},{0,28},{5,1},{9... | collective-permute-start | bytes 24584 | tf_op jit(solution)/shard_map/ppermute | solution.py:17
  13.3 0.7 copy-start.5
  14.8 6.7 %copy-start.3 = (f32[16,16,128]{2,1,0:T(8,128)S(1)}, f32[16,16,128]{2,1,0:T(8,128)}, u32[]{:S(2)}) copy-start(f32[16,16,128]{2,1,0:T(8,128)} %param.9) | copy-start | bytes 393220
  20.2 1.3 copy-start.2
  20.2 1.3 copy-start.1
  21.5 0.7 copy-start.4
  66.8 9.1 %collective-permute-start.4 = (f32[16,1,128]{2,0,1:T(8,128)S(1)}, f32[16,1,128]{2,0,1:T(8,128)S(1)}, u32[]{:S(2)}, u32[]{:S(2)}) collective-permute-start(f32[16,1,128]{2,0,1:T(8,128)S(1)} %bitcast.115), channel_id=1, source_target_pairs={{0,4},{4,8},{8,12},{12,16},{16,20},{20,24},{24,28},{28,0},{1,5},{5... | collective-permute-start | bytes 24584 | tf_op jit(solution)/shard_map/ppermute | solution.py:16
  69.1 6.8 %collective-permute-start.5 = (f32[16,1,128]{2,0,1:T(8,128)S(1)}, f32[16,1,128]{2,0,1:T(8,128)S(1)}, u32[]{:S(2)}, u32[]{:S(2)}) collective-permute-start(f32[16,1,128]{2,0,1:T(8,128)S(1)} %bitcast.113), channel_id=1, source_target_pairs={{4,0},{8,4},{12,8},{16,12},{20,16},{24,20},{28,24},{0,28},{5,1},{9... | collective-permute-start | bytes 24584 | tf_op jit(solution)/shard_map/ppermute | solution.py:17
  71.6 11.5 %collective-permute-start.6 = (f32[1,16,128]{2,1,0:T(8,128)S(1)}, f32[1,16,128]{2,1,0:T(8,128)S(1)}, u32[]{:S(2)}, u32[]{:S(2)}) collective-permute-start(f32[1,16,128]{2,1,0:T(8,128)S(1)} %get-tuple-element.41), channel_id=1, source_target_pairs={{1,0},{2,1},{3,2},{5,4},{6,5},{7,6},{9,8},{10,9},{11,10},{13,12},{... | collective-permute-start | bytes 24584 | tf_op jit(solution)/shard_map/ppermute | solution.py:17
  72.9 10.2 %collective-permute-start.7 = (f32[1,16,128]{2,1,0:T(8,128)S(1)}, f32[1,16,128]{2,1,0:T(8,128)S(1)}, u32[]{:S(2)}, u32[]{:S(2)}) collective-permute-start(f32[1,16,128]{2,1,0:T(8,128)S(1)} %get-tuple-element.42), channel_id=1, source_target_pairs={{0,1},{1,2},{2,3},{4,5},{5,6},{6,7},{8,9},{9,10},{10,11},{12,13},{... | collective-permute-start | bytes 24584 | tf_op jit(solution)/shard_map/ppermute | solution.py:16
  130.4 9.1 %collective-permute-start.8 = (f32[16,1,128]{2,0,1:T(8,128)S(1)}, f32[16,1,128]{2,0,1:T(8,128)S(1)}, u32[]{:S(2)}, u32[]{:S(2)}) collective-permute-start(f32[16,1,128]{2,0,1:T(8,128)S(1)} %bitcast.116), channel_id=1, source_target_pairs={{0,4},{4,8},{8,12},{12,16},{16,20},{20,24},{24,28},{28,0},{1,5},{5... | collective-permute-start | bytes 24584 | tf_op jit(solution)/shard_map/ppermute | solution.py:16
  132.7 6.8 %collective-permute-start.9 = (f32[16,1,128]{2,0,1:T(8,128)S(1)}, f32[16,1,128]{2,0,1:T(8,128)S(1)}, u32[]{:S(2)}, u32[]{:S(2)}) collective-permute-start(f32[16,1,128]{2,0,1:T(8,128)S(1)} %bitcast.114), channel_id=1, source_target_pairs={{4,0},{8,4},{12,8},{16,12},{20,16},{24,20},{28,24},{0,28},{5,1},{9... | collective-permute-start | bytes 24584 | tf_op jit(solution)/shard_map/ppermute | solution.py:17
  135.2 11.5 %collective-permute-start.10 = (f32[1,16,128]{2,1,0:T(8,128)S(1)}, f32[1,16,128]{2,1,0:T(8,128)S(1)}, u32[]{:S(2)}, u32[]{:S(2)}) collective-permute-start(f32[1,16,128]{2,1,0:T(8,128)S(1)} %get-tuple-element.35), channel_id=1, source_target_pairs={{1,0},{2,1},{3,2},{5,4},{6,5},{7,6},{9,8},{10,9},{11,10},{13,12},{... | collective-permute-start | bytes 24584 | tf_op jit(solution)/shard_map/ppermute | solution.py:17
  136.5 10.2 %collective-permute-start.11 = (f32[1,16,128]{2,1,0:T(8,128)S(1)}, f32[1,16,128]{2,1,0:T(8,128)S(1)}, u32[]{:S(2)}, u32[]{:S(2)}) collective-permute-start(f32[1,16,128]{2,1,0:T(8,128)S(1)} %get-tuple-element.36), channel_id=1, source_target_pairs={{0,1},{1,2},{2,3},{4,5},{5,6},{6,7},{8,9},{9,10},{10,11},{12,13},{... | collective-permute-start | bytes 24584 | tf_op jit(solution)/shard_map/ppermute | solution.py:16
where the time goes:
time: 244 us; the launch traced here: 243 us
  blocking collectives  175 us (72%)
  starting transfers between devices  28.6 us (12%)
  local copies, waits for them, and re-layouts  15.2 us (6%)
  other arithmetic  12.7 us (5%)
  between operations  9.45 us (4%)
    psum x3, blocking collectives, on_device(): totals = lax.psum(jnp.stack(terms), ('gx', 'gy')) / total_cells  116 us
    psum x1, blocking collectives, on_device(): lax.psum(local_product(residual, residual), ('gx', 'gy')) / total_cells  41.3 us
    all_gather x3, blocking collectives, on_device(): whole = lax.all_gather(edges, 'gy', axis=1, tiled=True)  17 us
    ppermute x6, starting transfers between devices, padded(): before = lax.ppermute(last, axis, up)  16.8 us
    ppermute x6, starting transfers between devices, padded(): after = lax.ppermute(initial, axis, down)  11.9 us
    another operation x2, local copies, waits for them, and re-layouts, on_device(): totals = lax.psum(jnp.stack(terms), ('gx', 'gy')) / total_cells  7.69 us
    reduce_sum x4, other arithmetic, local_product(): return jnp.sum(left * right)  4.94 us
  transfers between devices with their start and end apart: 12, of which 1 were waited for; matrix products, arithmetic and copies ran while one was open for 2% of the time, Pallas kernels for 0%

commit v1 on v0

--- a/solution.py
+++ b/solution.py
@@ -49,7 +49,14 @@
         pre = jnp.einsum("yxl,kl->yxk", residual, matrix, precision=lax.Precision.HIGHEST)
         wide = padded(pre, (("gx", 1),), 1, True)
         edges = jnp.stack([wide[:, 0], wide[:, -1]], 0)
-        whole = lax.all_gather(edges, "gy", axis=1, tiled=True)
+        ring = [edges]
+        for hop in range(3):
+            ring.append(lax.ppermute(ring[-1], "gy", [(dev, (dev + 1) % 4) for dev in range(4)]))
+        whole = jnp.roll(
+            jnp.concatenate(ring[::-1], axis=1),
+            (lax.axis_index("gy") + 1) * ring[0].shape[1],
+            axis=1,
+        )
         west_fix = jnp.take(whole[0], west_local, axis=0)
         east_fix = jnp.take(whole[1], east_local, axis=0)
         west = jnp.where(west_border, west_fix, edges[0])

time: 244 us -> 263 us (1.078)
  waiting for transfers between devices: 0.68 us -> 25.6 us
  blocking collectives: 175 us -> 164 us
  starting transfers between devices: 28.6 us -> 32.9 us
    ppermute x0 -> x9, waiting for transfers between devices: none -> 21.5 us  [on_device(): lax.ppermute(ring[-1], 'gy', [(dev, (dev + 1) % 4) for dev in range(4)])]
    all_gather x3 -> x0, blocking collectives: 17 us -> none  [on_device(): whole = lax.all_gather(edges, 'gy', axis=1, tiled=True)]
    psum x3, blocking collectives: 116 us -> 124 us  [on_device(): totals = lax.psum(jnp.stack(terms), ('gx', 'gy')) / total_cells]
    ppermute x6, starting transfers between devices: 16.8 us -> 20.4 us  [padded(): before = lax.ppermute(last, axis, up)]
    ppermute x6, waiting for transfers between devices: 0.66 us -> 4.02 us  [padded(): before = lax.ppermute(last, axis, up)]
  transfers between devices with their start and end apart: 12 -> 21, of which waited for: 1 -> 10; matrix products, arithmetic and copies ran while one was open for 2% -> 2% of each run, Pallas kernels for 0% -> 0%
where the time goes in v1:
time: 263 us; the launch traced here: 262 us
  blocking collectives  164 us (62%)
  starting transfers between devices  32.9 us (13%)
  waiting for transfers between devices  25.6 us (10%)
  local copies, waits for them, and re-layouts  15.2 us (6%)
  other arithmetic  13 us (5%)
  between operations  9.49 us (4%)
    psum x3, blocking collectives, on_device(): totals = lax.psum(jnp.stack(terms), ('gx', 'gy')) / total_cells  124 us
    psum x1, blocking collectives, on_device(): lax.psum(local_product(residual, residual), ('gx', 'gy')) / total_cells  40.3 us
    ppermute x9, waiting for transfers between devices, on_device(): lax.ppermute(ring[-1], 'gy', [(dev, (dev + 1) % 4) for dev in range(4)])  21.5 us
    ppermute x6, starting transfers between devices, padded(): before = lax.ppermute(last, axis, up)  20.4 us
    ppermute x6, starting transfers between devices, padded(): after = lax.ppermute(initial, axis, down)  11.9 us
    another operation x2, local copies, waits for them, and re-layouts, on_device(): totals = lax.psum(jnp.stack(terms), ('gx', 'gy')) / total_cells  7.69 us
  transfers between devices with their start and end apart: 21, of which 10 were waited for; matrix products, arithmetic and copies ran while one was open for 2% of the time, Pallas kernels for 0%

profile of v1, /device:TPU:0, one launch (start us, length us, event | category | flops | bytes accessed | tf_op | source)
XLA Modules:
  0.0 262.3 jit_solution(15212935974371005907)
XLA Ops:
  0.7 0.9 copy-done
  1.5 1.2 convolution_bitcast_fusion
  2.7 1.3 collective-permute-start.5
  4.0 3.0 %collective-permute-start.6 = (f32[1,16,128]{2,1,0:T(8,128)S(1)}, f32[1,16,128]{2,1,0:T(8,128)S(1)}, u32[]{:S(2)}, u32[]{:S(2)}) collective-permute-start(f32[1,16,128]{2,1,0:T(8,128)S(1)} %get-tuple-element.49), channel_id=1, source_target_pairs={{0,1},{1,2},{2,3},{4,5},{5,6},{6,7},{8,9},{9,10},{10,11},{12,13},{... | collective-permute-start | bytes 24584 | tf_op jit(solution)/shard_map/ppermute | solution.py:16
  7.1 3.0 %collective-permute-start = (f32[16,1,128]{2,0,1:T(8,128)S(1)}, f32[16,1,128]{2,0,1:T(8,128)S(1)}, u32[]{:S(2)}, u32[]{:S(2)}) collective-permute-start(f32[16,1,128]{2,0,1:T(8,128)S(1)} %bitcast.118), channel_id=1, source_target_pairs={{0,4},{4,8},{8,12},{12,16},{16,20},{20,24},{24,28},{28,0},{1,5},{5... | collective-permute-start | bytes 24584 | tf_op jit(solution)/shard_map/ppermute | solution.py:16
  10.1 3.1 %collective-permute-start.1 = (f32[16,1,128]{2,0,1:T(8,128)S(1)}, f32[16,1,128]{2,0,1:T(8,128)S(1)}, u32[]{:S(2)}, u32[]{:S(2)}) collective-permute-start(f32[16,1,128]{2,0,1:T(8,128)S(1)} %bitcast.117), channel_id=1, source_target_pairs={{4,0},{8,4},{12,8},{16,12},{20,16},{24,20},{28,24},{0,28},{5,1},{9... | collective-permute-start | bytes 24584 | tf_op jit(solution)/shard_map/ppermute | solution.py:17
  13.3 0.7 copy-done.5
  14.0 0.1 compare_and_fusion
  14.0 0.8 collective-permute-done
  14.8 0.2 collective-permute-start.2
  15.1 2.9 %collective-permute-done.2 = f32[2,16,128]{2,1,0:T(8,128)S(1)} collective-permute-done((f32[2,16,128]{2,1,0:T(8,128)S(1)}, f32[2,16,128]{2,1,0:T(8,128)S(1)}, u32[]{:S(2)}, u32[]{:S(2)}) %collective-permute-start.2) | collective-permute-done | bytes 16416 | tf_op jit(solution)/shard_map/ppermute | solution.py:54
  18.0 0.1 compare_and_fusion.1
  18.1 3.1 %collective-permute-done.3 = f32[2,16,128]{2,1,0:T(8,128)S(1)} collective-permute-done((f32[2,16,128]{2,1,0:T(8,128)S(1)}, f32[2,16,128]{2,1,0:T(8,128)S(1)}, u32[]{:S(2)}, u32[]{:S(2)}) %collective-permute-start.3) | collective-permute-done | bytes 16416 | tf_op jit(solution)/shard_map/ppermute | solution.py:54
  21.2 3.1 %collective-permute-done.4 = f32[2,16,128]{2,1,0:T(8,128)S(1)} collective-permute-done((f32[2,16,128]{2,1,0:T(8,128)S(1)}, f32[2,16,128]{2,1,0:T(8,128)S(1)}, u32[]{:S(2)}, u32[]{:S(2)}) %collective-permute-start.4) | collective-permute-done | bytes 16416 | tf_op jit(solution)/shard_map/ppermute | solution.py:54
  24.3 0.1 fusion.48
  24.4 0.6 gather_fusion
  25.0 0.6 gather_fusion.1
  25.6 0.1 bitcast_select_fusion.5
  25.8 0.6 copy-done.4
  26.4 0.7 multiply_reduce_fusion.14
  27.1 1.4 pad_maximum_fusion.9
  28.5 40.3 %psum.28 = f32[2]{0:T(128)S(1)} all-reduce(f32[2]{0:T(128)S(1)} %pad_maximum_fusion.9), channel_id=1, replica_groups=mesh['gx'=8,'gy'=4] {'gx','gy'}, use_global_device_ids=true, to_apply=%region_2.5 | all-reduce | flops 2 | bytes 16 | tf_op jit(solution)/shard_map/psum | solution.py:77
  68.8 0.6 fusion.81
  70.7 0.3 fusion.56
  71.0 2.3 collective-permute-start.7
  73.4 2.5 collective-permute-start.8
  75.8 1.6 collective-permute-done.7
  77.5 3.2 %collective-permute-done.9 = f32[2,16,128]{2,1,0:T(8,128)S(1)} collective-permute-done((f32[2,16,128]{2,1,0:T(8,128)S(1)}, f32[2,16,128]{2,1,0:T(8,128)S(1)}, u32[]{:S(2)}, u32[]{:S(2)}) %collective-permute-start.9) | collective-permute-done | bytes 16416 | tf_op jit(solution)/shard_map/ppermute | solution.py:54
  80.6 0.1 collective-permute-start.10
  80.7 3.0 %collective-permute-done.10 = f32[2,16,128]{2,1,0:T(8,128)S(1)} collective-permute-done((f32[2,16,128]{2,1,0:T(8,128)S(1)}, f32[2,16,128]{2,1,0:T(8,128)S(1)}, u32[]{:S(2)}, u32[]{:S(2)}) %collective-permute-start.10) | collective-permute-done | bytes 16416 | tf_op jit(solution)/shard_map/ppermute | solution.py:54
  83.8 0.1 collective-permute-start.11
  83.9 1.3 collective-permute-start.12
  85.2 4.8 %collective-permute-start.13 = (f32[1,16,128]{2,1,0:T(8,128)S(1)}, f32[1,16,128]{2,1,0:T(8,128)S(1)}, u32[]{:S(2)}, u32[]{:S(2)}) collective-permute-start(f32[1,16,128]{2,1,0:T(8,128)S(1)} %get-tuple-element.43), channel_id=1, source_target_pairs={{0,1},{1,2},{2,3},{4,5},{5,6},{6,7},{8,9},{9,10},{10,11},{12,13},{... | collective-permute-start | bytes 24584 | tf_op jit(solution)/shard_map/ppermute | solution.py:16
  90.0 0.1 fusion.39
  90.1 0.6 gather_fusion.2
  90.7 0.6 gather_fusion.3
  91.3 0.1 bitcast_select_fusion.3
  91.4 0.8 multiply_reduce_fusion.8
  92.2 3.2 %stack.76 = f32[5]{0:T(128)S(1)} concatenate(f32[1]{0:T(128)} %bitcast.28, f32[1]{0:T(128)} %bitcast.29, f32[1]{0:T(128)} %bitcast.30, f32[1]{0:T(128)} %bitcast.31, f32[1]{0:T(128)} %bitcast.32), dimensions={0} | concatenate | bytes 40 | tf_op jit(solution)/shard_map/stack | solution.py:77
  95.4 41.9 %psum.29 = f32[5]{0:T(128)S(1)} all-reduce(f32[5]{0:T(128)S(1)} %stack.76), channel_id=1, replica_groups=mesh['gx'=8,'gy'=4] {'gx','gy'}, use_global_device_ids=true, to_apply=%region_8.11 | all-reduce | flops 5 | bytes 40 | tf_op jit(solution)/shard_map/psum | solution.py:77
  137.3 0.6 fusion.79
  141.8 0.7 multiply_subtract_fusion.1
  142.5 0.3 fusion.54
  142.8 2.3 collective-permute-start.14
  145.1 2.5 collective-permute-start.15
  147.6 1.6 collective-permute-done.14
  149.2 3.2 %collective-permute-done.16 = f32[2,16,128]{2,1,0:T(8,128)S(1)} collective-permute-done((f32[2,16,128]{2,1,0:T(8,128)S(1)}, f32[2,16,128]{2,1,0:T(8,128)S(1)}, u32[]{:S(2)}, u32[]{:S(2)}) %collective-permute-start.16) | collective-permute-done | bytes 16416 | tf_op jit(solution)/shard_map/ppermute | solution.py:54
  152.4 0.1 collective-permute-start.17
  152.5 3.0 %collective-permute-done.17 = f32[2,16,128]{2,1,0:T(8,128)S(1)} collective-permute-done((f32[2,16,128]{2,1,0:T(8,128)S(1)}, f32[2,16,128]{2,1,0:T(8,128)S(1)}, u32[]{:S(2)}, u32[]{:S(2)}) %collective-permute-start.17) | collective-permute-done | bytes 16416 | tf_op jit(solution)/shard_map/ppermute | solution.py:54
  155.5 0.1 collective-permute-start.18
  155.6 1.3 collective-permute-start.19
  156.9 4.8 %collective-permute-start.20 = (f32[1,16,128]{2,1,0:T(8,128)S(1)}, f32[1,16,128]{2,1,0:T(8,128)S(1)}, u32[]{:S(2)}, u32[]{:S(2)}) collective-permute-start(f32[1,16,128]{2,1,0:T(8,128)S(1)} %get-tuple-element.37), channel_id=1, source_target_pairs={{0,1},{1,2},{2,3},{4,5},{5,6},{6,7},{8,9},{9,10},{10,11},{12,13},{... | collective-permute-start | bytes 24584 | tf_op jit(solution)/shard_map/ppermute | solution.py:16
  161.8 0.1 fusion.30
  161.9 0.6 gather_fusion.4
  162.5 0.6 gather_fusion.5
  163.2 0.9 multiply_reduce_fusion.1
  164.1 4.5 %stack.85 = f32[7]{0:T(128)S(1)} concatenate(f32[1]{0:T(128)} %bitcast.46, f32[1]{0:T(128)} %bitcast.47, f32[1]{0:T(128)} %bitcast.48, f32[1]{0:T(128)} %bitcast.49, f32[1]{0:T(128)} %bitcast.50, f32[1]{0:T(128)} %bitcast.51, f32[1]{0:T(128)} %bitcast.52), dimensions={0} | concatenate | bytes 56 | tf_op jit(solution)/shard_map/stack | solution.py:77
  168.5 41.9 %psum.30 = f32[7]{0:T(128)S(1)} all-reduce(f32[7]{0:T(128)S(1)} %stack.85), channel_id=1, replica_groups=mesh['gx'=8,'gy'=4] {'gx','gy'}, use_global_device_ids=true, to_apply=%region_16.19 | all-reduce | flops 7 | bytes 56 | tf_op jit(solution)/shard_map/psum | solution.py:77
  210.4 0.8 multiply_reduce_fusion.16
  211.2 0.7 fusion.80
  214.4 2.6 multiply_add_fusion
  217.0 2.5 multiply_reduce_fusion
  219.5 40.3 %psum.31 = f32[]{:T(128)} all-reduce(f32[]{:T(128)} %get-tuple-element.21), channel_id=1, replica_groups=mesh['gx'=8,'gy'=4] {'gx','gy'}, use_global_device_ids=true, to_apply=%region_20.23 | all-reduce | flops 1 | bytes 8 | tf_op jit(solution)/shard_map/psum | solution.py:95
  260.5 1.8 pad_maximum_fusion.10
  (50 shorter events, 0.5 us)
Async XLA Ops:
  0.6 0.9 copy-start
  2.7 23.0 %collective-permute-start.5 = (f32[1,16,128]{2,1,0:T(8,128)S(1)}, f32[1,16,128]{2,1,0:T(8,128)S(1)}, u32[]{:S(2)}, u32[]{:S(2)}) collective-permute-start(f32[1,16,128]{2,1,0:T(8,128)S(1)} %get-tuple-element.48), channel_id=1, source_target_pairs={{1,0},{2,1},{3,2},{5,4},{6,5},{7,6},{9,8},{10,9},{11,10},{13,12},{... | collective-permute-start | bytes 24584 | tf_op jit(solution)/shard_map/ppermute | solution.py:17
  4.0 21.7 %collective-permute-start.6 = (f32[1,16,128]{2,1,0:T(8,128)S(1)}, f32[1,16,128]{2,1,0:T(8,128)S(1)}, u32[]{:S(2)}, u32[]{:S(2)}) collective-permute-start(f32[1,16,128]{2,1,0:T(8,128)S(1)} %get-tuple-element.49), channel_id=1, source_target_pairs={{0,1},{1,2},{2,3},{4,5},{5,6},{6,7},{8,9},{9,10},{10,11},{12,13},{... | collective-permute-start | bytes 24584 | tf_op jit(solution)/shard_map/ppermute | solution.py:16
  7.1 7.7 %collective-permute-start = (f32[16,1,128]{2,0,1:T(8,128)S(1)}, f32[16,1,128]{2,0,1:T(8,128)S(1)}, u32[]{:S(2)}, u32[]{:S(2)}) collective-permute-start(f32[16,1,128]{2,0,1:T(8,128)S(1)} %bitcast.118), channel_id=1, source_target_pairs={{0,4},{4,8},{8,12},{12,16},{16,20},{20,24},{24,28},{28,0},{1,5},{5... | collective-permute-start | bytes 24584 | tf_op jit(solution)/shard_map/ppermute | solution.py:16
  10.1 4.7 %collective-permute-start.1 = (f32[16,1,128]{2,0,1:T(8,128)S(1)}, f32[16,1,128]{2,0,1:T(8,128)S(1)}, u32[]{:S(2)}, u32[]{:S(2)}) collective-permute-start(f32[16,1,128]{2,0,1:T(8,128)S(1)} %bitcast.117), channel_id=1, source_target_pairs={{4,0},{8,4},{12,8},{16,12},{20,16},{24,20},{28,24},{0,28},{5,1},{9... | collective-permute-start | bytes 24584 | tf_op jit(solution)/shard_map/ppermute | solution.py:17
  13.3 0.7 copy-start.5
  14.8 3.2 %collective-permute-start.2 = (f32[2,16,128]{2,1,0:T(8,128)S(1)}, f32[2,16,128]{2,1,0:T(8,128)S(1)}, u32[]{:S(2)}, u32[]{:S(2)}) collective-permute-start(f32[2,16,128]{2,1,0:T(8,128)S(1)} %pad_maximum_fusion.6), channel_id=1, source_target_pairs={{0,1},{1,2},{2,3},{3,0},{4,5},{5,6},{6,7},{7,4},{8,9},{9,10},{10,1... | collective-permute-start | bytes 49160 | tf_op jit(solution)/shard_map/ppermute | solution.py:54
  18.0 3.2 %collective-permute-start.3 = (f32[2,16,128]{2,1,0:T(8,128)S(1)}, f32[2,16,128]{2,1,0:T(8,128)S(1)}, u32[]{:S(2)}, u32[]{:S(2)}) collective-permute-start(f32[2,16,128]{2,1,0:T(8,128)S(1)} %collective-permute-done.2), channel_id=1, source_target_pairs={{0,1},{1,2},{2,3},{3,0},{4,5},{5,6},{6,7},{7,4},{8,9},{9,10},{10,1... | collective-permute-start | bytes 49160 | tf_op jit(solution)/shard_map/ppermute | solution.py:54
  21.2 3.2 %collective-permute-start.4 = (f32[2,16,128]{2,1,0:T(8,128)S(1)}, f32[2,16,128]{2,1,0:T(8,128)S(1)}, u32[]{:S(2)}, u32[]{:S(2)}) collective-permute-start(f32[2,16,128]{2,1,0:T(8,128)S(1)} %collective-permute-done.3), channel_id=1, source_target_pairs={{0,1},{1,2},{2,3},{3,0},{4,5},{5,6},{6,7},{7,4},{8,9},{9,10},{10,1... | collective-permute-start | bytes 49160 | tf_op jit(solution)/shard_map/ppermute | solution.py:54
  24.3 1.4 copy-start.3
  24.4 1.4 copy-start.2
  24.4 1.3 copy-start.1
  25.7 0.7 copy-start.4
  71.0 6.4 %collective-permute-start.7 = (f32[16,1,128]{2,0,1:T(8,128)S(1)}, f32[16,1,128]{2,0,1:T(8,128)S(1)}, u32[]{:S(2)}, u32[]{:S(2)}) collective-permute-start(f32[16,1,128]{2,0,1:T(8,128)S(1)} %bitcast.121), channel_id=1, source_target_pairs={{0,4},{4,8},{8,12},{12,16},{16,20},{20,24},{24,28},{28,0},{1,5},{5... | collective-permute-start | bytes 24584 | tf_op jit(solution)/shard_map/ppermute | solution.py:16
  73.4 4.1 %collective-permute-start.8 = (f32[16,1,128]{2,0,1:T(8,128)S(1)}, f32[16,1,128]{2,0,1:T(8,128)S(1)}, u32[]{:S(2)}, u32[]{:S(2)}) collective-permute-start(f32[16,1,128]{2,0,1:T(8,128)S(1)} %bitcast.119), channel_id=1, source_target_pairs={{4,0},{8,4},{12,8},{16,12},{20,16},{24,20},{28,24},{0,28},{5,1},{9... | collective-permute-start | bytes 24584 | tf_op jit(solution)/shard_map/ppermute | solution.py:17
  77.4 3.2 %collective-permute-start.9 = (f32[2,16,128]{2,1,0:T(8,128)S(1)}, f32[2,16,128]{2,1,0:T(8,128)S(1)}, u32[]{:S(2)}, u32[]{:S(2)}) collective-permute-start(f32[2,16,128]{2,1,0:T(8,128)S(1)} %pad_maximum_fusion.7), channel_id=1, source_target_pairs={{0,1},{1,2},{2,3},{3,0},{4,5},{5,6},{6,7},{7,4},{8,9},{9,10},{10,1... | collective-permute-start | bytes 49160 | tf_op jit(solution)/shard_map/ppermute | solution.py:54
  80.6 3.2 %collective-permute-start.10 = (f32[2,16,128]{2,1,0:T(8,128)S(1)}, f32[2,16,128]{2,1,0:T(8,128)S(1)}, u32[]{:S(2)}, u32[]{:S(2)}) collective-permute-start(f32[2,16,128]{2,1,0:T(8,128)S(1)} %collective-permute-done.9), channel_id=1, source_target_pairs={{0,1},{1,2},{2,3},{3,0},{4,5},{5,6},{6,7},{7,4},{8,9},{9,10},{10,1... | collective-permute-start | bytes 49160 | tf_op jit(solution)/shard_map/ppermute | solution.py:54
  83.8 6.2 %collective-permute-start.11 = (f32[2,16,128]{2,1,0:T(8,128)S(1)}, f32[2,16,128]{2,1,0:T(8,128)S(1)}, u32[]{:S(2)}, u32[]{:S(2)}) collective-permute-start(f32[2,16,128]{2,1,0:T(8,128)S(1)} %collective-permute-done.10), channel_id=1, source_target_pairs={{0,1},{1,2},{2,3},{3,0},{4,5},{5,6},{6,7},{7,4},{8,9},{9,10},{10,1... | collective-permute-start | bytes 49160 | tf_op jit(solution)/shard_map/ppermute | solution.py:54
  83.9 7.5 %collective-permute-start.12 = (f32[1,16,128]{2,1,0:T(8,128)S(1)}, f32[1,16,128]{2,1,0:T(8,128)S(1)}, u32[]{:S(2)}, u32[]{:S(2)}) collective-permute-start(f32[1,16,128]{2,1,0:T(8,128)S(1)} %get-tuple-element.42), channel_id=1, source_target_pairs={{1,0},{2,1},{3,2},{5,4},{6,5},{7,6},{9,8},{10,9},{11,10},{13,12},{... | collective-permute-start | bytes 24584 | tf_op jit(solution)/shard_map/ppermute | solution.py:17
  85.2 6.3 %collective-permute-start.13 = (f32[1,16,128]{2,1,0:T(8,128)S(1)}, f32[1,16,128]{2,1,0:T(8,128)S(1)}, u32[]{:S(2)}, u32[]{:S(2)}) collective-permute-start(f32[1,16,128]{2,1,0:T(8,128)S(1)} %get-tuple-element.43), channel_id=1, source_target_pairs={{0,1},{1,2},{2,3},{4,5},{5,6},{6,7},{8,9},{9,10},{10,11},{12,13},{... | collective-permute-start | bytes 24584 | tf_op jit(solution)/shard_map/ppermute | solution.py:16
  142.8 6.4 %collective-permute-start.14 = (f32[16,1,128]{2,0,1:T(8,128)S(1)}, f32[16,1,128]{2,0,1:T(8,128)S(1)}, u32[]{:S(2)}, u32[]{:S(2)}) collective-permute-start(f32[16,1,128]{2,0,1:T(8,128)S(1)} %bitcast.122), channel_id=1, source_target_pairs={{0,4},{4,8},{8,12},{12,16},{16,20},{20,24},{24,28},{28,0},{1,5},{5... | collective-permute-start | bytes 24584 | tf_op jit(solution)/shard_map/ppermute | solution.py:16
  145.1 4.1 %collective-permute-start.15 = (f32[16,1,128]{2,0,1:T(8,128)S(1)}, f32[16,1,128]{2,0,1:T(8,128)S(1)}, u32[]{:S(2)}, u32[]{:S(2)}) collective-permute-start(f32[16,1,128]{2,0,1:T(8,128)S(1)} %bitcast.120), channel_id=1, source_target_pairs={{4,0},{8,4},{12,8},{16,12},{20,16},{24,20},{28,24},{0,28},{5,1},{9... | collective-permute-start | bytes 24584 | tf_op jit(solution)/shard_map/ppermute | solution.py:17
  149.2 3.2 %collective-permute-start.16 = (f32[2,16,128]{2,1,0:T(8,128)S(1)}, f32[2,16,128]{2,1,0:T(8,128)S(1)}, u32[]{:S(2)}, u32[]{:S(2)}) collective-permute-start(f32[2,16,128]{2,1,0:T(8,128)S(1)} %pad_maximum_fusion.8), channel_id=1, source_target_pairs={{0,1},{1,2},{2,3},{3,0},{4,5},{5,6},{6,7},{7,4},{8,9},{9,10},{10,1... | collective-permute-start | bytes 49160 | tf_op jit(solution)/shard_map/ppermute | solution.py:54
  152.4 3.2 %collective-permute-start.17 = (f32[2,16,128]{2,1,0:T(8,128)S(1)}, f32[2,16,128]{2,1,0:T(8,128)S(1)}, u32[]{:S(2)}, u32[]{:S(2)}) collective-permute-start(f32[2,16,128]{2,1,0:T(8,128)S(1)} %collective-permute-done.16), channel_id=1, source_target_pairs={{0,1},{1,2},{2,3},{3,0},{4,5},{5,6},{6,7},{7,4},{8,9},{9,10},{10,1... | collective-permute-start | bytes 49160 | tf_op jit(solution)/shard_map/ppermute | solution.py:54
  155.5 6.2 %collective-permute-start.18 = (f32[2,16,128]{2,1,0:T(8,128)S(1)}, f32[2,16,128]{2,1,0:T(8,128)S(1)}, u32[]{:S(2)}, u32[]{:S(2)}) collective-permute-start(f32[2,16,128]{2,1,0:T(8,128)S(1)} %collective-permute-done.17), channel_id=1, source_target_pairs={{0,1},{1,2},{2,3},{3,0},{4,5},{5,6},{6,7},{7,4},{8,9},{9,10},{10,1... | collective-permute-start | bytes 49160 | tf_op jit(solution)/shard_map/ppermute | solution.py:54
  155.6 7.5 %collective-permute-start.19 = (f32[1,16,128]{2,1,0:T(8,128)S(1)}, f32[1,16,128]{2,1,0:T(8,128)S(1)}, u32[]{:S(2)}, u32[]{:S(2)}) collective-permute-start(f32[1,16,128]{2,1,0:T(8,128)S(1)} %get-tuple-element.36), channel_id=1, source_target_pairs={{1,0},{2,1},{3,2},{5,4},{6,5},{7,6},{9,8},{10,9},{11,10},{13,12},{... | collective-permute-start | bytes 24584 | tf_op jit(solution)/shard_map/ppermute | solution.py:17
  156.9 6.3 %collective-permute-start.20 = (f32[1,16,128]{2,1,0:T(8,128)S(1)}, f32[1,16,128]{2,1,0:T(8,128)S(1)}, u32[]{:S(2)}, u32[]{:S(2)}) collective-permute-start(f32[1,16,128]{2,1,0:T(8,128)S(1)} %get-tuple-element.37), channel_id=1, source_target_pairs={{0,1},{1,2},{2,3},{4,5},{5,6},{6,7},{8,9},{9,10},{10,11},{12,13},{... | collective-permute-start | bytes 24584 | tf_op jit(solution)/shard_map/ppermute | solution.py:16
